TPU v7x, 32 devices: a whole 2x2x4 slice. The times are simulated.
32 devices in a mesh: comp: 8 (over y, x, core), tile: 4 (over z).
Axes of the slice: x: 2, y: 2, z: 4, core: 2. Of those that a mesh axis runs over, the one named last changes fastest.
Arguments:
- atm_state: float32 [128, 128, 512], P(None, 'comp', 'tile'), may hold values from -6 to 6
- ocean_state: float32 [48, 128, 512], P(None, 'comp', 'tile'), may hold values from -6 to 6
- atm_rate: float32 [128], replicated, may hold values from 0.02 to 0.24
- ocean_rate: float32 [48], replicated, may hold values from 0.02 to 0.24
- ocean_mask: int32 [128, 4], P('comp', 'tile'), may hold values 0 or 1
- remap_weight: bfloat16 [8, 192, 128, 128], P('comp', 'tile'), may hold values from -0.5 to 0.5
- pair_src: int32 [8, 192], P('comp', 'tile'), may hold values from 0 to 63, as said below
- pair_tgt: int32 [8, 192], P('comp', 'tile'), may hold values from 0 to 63, as said below
- pair_count: int32 [8, 4], P('comp', 'tile'), may hold values from 24 to 48, as said below
Outputs:
- atm_next: float32 [128, 128, 512], P(None, 'comp', 'tile')
- ocean_next: float32 [48, 128, 512], P(None, 'comp', 'tile')
Inputs may be any that keep to these rules, and one draw needn't show every extreme that they name: `pair_src`: entry d * 48 + j of row b names atmosphere tile e * 16 + y of band b. Among the first pair_count[b, d] entries of device d at most 13 have the same e, and every device has 13 live entries with one same e. `pair_tgt`: entry d * 48 + j of row b names ocean tile e * 16 + y of band b. Among the first pair_count[b, d] entries of device d at most 13 have the same e, and every device has 13 live entries with one same e. `pair_count`: each row b has some device with 48 live slots.
All inputs are finite; a program needn't handle non-finite values. No bound on the sum of `ocean_mask` on one device may be relied on, other than what follows from the above.
Results may differ from a plain program's by a relative error of at most 0.002.
Values may be sent and summed in bfloat16 or wider, within the bound.
No kernel may reach another device: no remote copies, remote signals or barrier semaphores. Data moves between devices by JAX's collectives and lax.ppermute only.
A program may use at most 64 MiB of HBM per device.

v0:
```python
import jax
import jax.numpy as jnp
from jax import lax
from jax.sharding import PartitionSpec as P

SURF = 8


def padded_2(block, sides, width):
    for axis, dim in sides:
        count = lax.axis_size(axis)
        forward = [(i, i + 1) for i in range(count - 1)]
        forward.append((count - 1, 0))
        backward = [(target, source) for source, target in forward]
        low = lax.ppermute(
            lax.slice_in_dim(block, block.shape[dim] - width, None, axis=dim), axis, forward
        )
        high = lax.ppermute(lax.slice_in_dim(block, 0, width, axis=dim), axis, backward)
        block = jnp.concatenate([low, block, high], axis=dim)
    return block


def relax(padded, spread):
    center = padded[:, 1:-1, 1:-1]
    beside_all = (
        padded[:, 2:, 1:-1] + padded[:, :-2, 1:-1] + padded[:, 1:-1, 2:] + padded[:, 1:-1, :-2]
    )
    return center + spread[:, None, None] * (beside_all - 4.0 * center)


def ghosts(padded, width):
    row_total = padded.shape[1]
    row_index = jnp.arange(row_total)
    position = lax.axis_index("comp")
    at_first = jnp.logical_and(row_index < width, position == 0)
    at_last = jnp.logical_and(row_index >= row_total - width, position == lax.axis_size("comp") - 1)
    retain = jnp.logical_not(jnp.logical_or(at_first, at_last)).astype(jnp.float32)
    return padded * retain[None, :, None]


def shards(
    atm_state,
    ocean_state,
    atm_rate,
    ocean_rate,
    ocean_mask,
    remap_weight,
    pair_src,
    pair_tgt,
    pair_count,
):
    atm_rows = atm_state.shape[1]
    ocean_rows = ocean_state.shape[1]
    cell_total = atm_state.shape[2]
    pair_total = pair_src.shape[1]
    wet_rows = ocean_mask[:, 0].astype(jnp.float32)
    atm_source = atm_state[:SURF].astype(jnp.bfloat16)
    ocean_source = (ocean_state[:SURF] * wet_rows[None, :, None]).astype(jnp.bfloat16)
    atm_band, ocean_band = (
        lax.all_gather(atm_source, "tile", axis=1, tiled=True),
        lax.all_gather(ocean_source, "tile", axis=1, tiled=True),
    )
    anchor = pair_src[0]
    target = pair_tgt[0]
    active = jnp.arange(pair_total) < pair_count[0, 0]
    active_float = active.astype(jnp.float32)[:, None, None]
    weights = remap_weight[0]
    forward = (
        jnp.einsum(
            "fpt,pts->pfs",
            jnp.take(atm_band, anchor, axis=1),
            weights,
            preferred_element_type=jnp.float32,
        )
        * active_float
    )
    reverse = (
        jnp.einsum(
            "fps,pts->pft",
            jnp.take(ocean_band, target, axis=1),
            weights,
            preferred_element_type=jnp.float32,
        )
        * active_float
    )
    band_rows = atm_rows + ocean_rows
    ahead_codes = jnp.where(
        active, target // ocean_rows * band_rows + atm_rows + target % ocean_rows, -1
    )
    back_codes = jnp.where(active, anchor // atm_rows * band_rows + anchor % atm_rows, -1)
    ahead_flat = forward.reshape(pair_total, -1)
    back_flat = reverse.reshape(pair_total, -1)
    row_codes = jnp.arange(band_rows * lax.axis_size("tile"))
    ahead_hot = (row_codes[:, None] == ahead_codes[None, :]).astype(jnp.float32)
    back_hot = (row_codes[:, None] == back_codes[None, :]).astype(jnp.float32)
    summed = lax.psum_scatter(
        jnp.dot(
            ahead_hot,
            ahead_flat,
            precision=lax.Precision.HIGHEST,
            preferred_element_type=jnp.float32,
        )
        + jnp.dot(
            back_hot, back_flat, precision=lax.Precision.HIGHEST, preferred_element_type=jnp.float32
        ),
        "tile",
        scatter_dimension=0,
        tiled=True,
    )
    atm_force = summed[:atm_rows].reshape(atm_rows, SURF, cell_total)
    ocean_force = summed[atm_rows:].reshape(ocean_rows, SURF, cell_total)
    atm_padded = ghosts(padded_2(atm_state, (("comp", 1), ("tile", 2)), 2), 2)
    atm_stepped = relax(ghosts(relax(atm_padded, atm_rate), 1), atm_rate)
    ocean_padded = ghosts(padded_2(ocean_state, (("comp", 1), ("tile", 2)), 2), 2)
    ocean_stepped = relax(ghosts(relax(ocean_padded, ocean_rate), 1), ocean_rate)
    atm_next = atm_stepped.at[:SURF].add(jnp.transpose(atm_force, (1, 0, 2)))
    ocean_next = ocean_stepped.at[:SURF].add(
        jnp.transpose(ocean_force, (1, 0, 2)) * wet_rows[None, :, None]
    )
    return (atm_next, ocean_next)


def solution(mesh):
    return jax.shard_map(
        shards,
        mesh=mesh,
        in_specs=(
            P(None, "comp", "tile"),
            P(None, "comp", "tile"),
            P(),
            P(),
            P("comp", "tile"),
            P("comp", "tile", None, None),
            P("comp", "tile"),
            P("comp", "tile"),
            P("comp", "tile"),
        ),
        out_specs=(P(None, "comp", "tile"), P(None, "comp", "tile")),
        check_vma=False,
    )
```

profile of v0, /device:TPU:0, one launch (start us, length us, event | category | flops | bytes accessed | tf_op | source)
XLA Modules:
  0.0 102.0 jit_solution(3758282511293976926)
XLA Ops:
  7.3 2.0 %copy.67 = f32[128,16,128]{0,1,2:T(8,128)S(1)} copy(f32[128,16,128]{2,1,0:T(8,128)} %param.15) | data formatting | bytes 2097152 | tf_op args[0]
  10.6 2.9 %collective-permute-start.1 = (f32[128,2,128]{0,1,2:T(2,128)}, f32[128,2,128]{0,1,2:T(2,128)}, u32[]{:S(2)}, u32[]{:S(2)}) collective-permute-start(f32[128,2,128]{0,1,2:T(2,128)} %get-tuple-element.38), channel_id=1, source_target_pairs={{4,0},{8,4},{12,8},{16,12},{20,16},{24,20},{28,24},{0,28},{5,1},{9... | collective-permute-start | bytes 393224 | tf_op jit(solution)/shard_map/ppermute | solution.py:18
  15.0 14.4 %all_gather.6 = bf16[8,64,128]{2,0,1:T(8,128)(2,1)S(1)} all-gather(bf16[8,16,128]{2,0,1:T(8,128)(2,1)S(1)} %copy.100), channel_id=1, replica_groups=mesh['comp'=8,'tile'=4] {'tile'}, dimensions={1}, use_global_device_ids=true | all-gather | bytes 163840 | tf_op jit(solution)/shard_map/all_gather | solution.py:60
  30.9 14.3 %all_gather.7 = bf16[8,64,128]{2,0,1:T(8,128)(2,1)} all-gather(bf16[8,16,128]{2,0,1:T(8,128)(2,1)S(1)} %fusion.36), channel_id=1, replica_groups=mesh['comp'=8,'tile'=4] {'tile'}, dimensions={1}, use_global_device_ids=true | all-gather | bytes 163840 | tf_op jit(solution)/shard_map/all_gather | solution.py:61
  47.4 2.1 %gather_fusion.1 = bf16[48,8,128]{2,1,0:T(8,128)(2,1)} fusion(bf16[8,64,128]{2,0,1:T(8,128)(2,1)} %all_gather.7, s32[1024]{0:T(1024)S(1)} %pad_clamp_fusion), kind=kCustom, calls=%fused_computation.1.clone | custom fusion | bytes 196800 | tf_op jit(solution)/shard_map/jit(_take)/gather | solution.py:80
  49.6 1.8 %fusion.11 = f32[48,8,128]{2,1,0:T(8,128)S(1)} fusion(bf16[1,48,128,128]{3,2,1,0:T(8,128)(2,1)S(1)} %copy-done, bf16[48,8,128]{2,1,0:T(8,128)(2,1)} %gather_fusion.1, f32[48]{0:T(128)S(1)} %compare_convert_fusion, pred[48]{0:T(512)(128)(4,1)S(1)} %compare_and_fusion), kind=kOutput, calls=%fused_computation.17 | convolution fusion | flops 12681216 | bytes 1868016 | tf_op jit(solution)/shard_map/fps,pts->pft/dot_general | solution.py:78
  51.4 1.9 %convolution_add_fusion = f32[128,1024]{1,0:T(8,128)} fusion(f32[128,1024]{1,0:T(8,128)S(1)} %fusion.26, f32[6,8,8,128]{3,2,1,0:T(8,128)S(1)} %bitcast.52, s32[48]{0:T(128)} %fusion.44), kind=kOutput, calls=%fused_computation.15 | convolution fusion | flops 75634688 | bytes 1245376 | tf_op jit(solution)/shard_map/dot_general | solution.py:103
  53.3 1.4 %fusion.50 = (f32[48,2,128]{2,0,1:T(8,128)}, f32[48,2,128]{2,0,1:T(8,128)S(1)}) fusion(f32[48,16,128]{2,0,1:T(8,128)} %copy-done.2), kind=kLoop, calls=%fused_computation.98 | loop fusion | bytes 196608 | tf_op jit(solution)/shard_map/slice | solution.py:18
  54.8 2.6 %collective-permute-start.5 = (f32[48,2,128]{2,0,1:T(8,128)}, f32[48,2,128]{2,0,1:T(8,128)}, u32[]{:S(2)}, u32[]{:S(2)}) collective-permute-start(f32[48,2,128]{2,0,1:T(8,128)} %get-tuple-element.41), channel_id=1, source_target_pairs={{4,0},{8,4},{12,8},{16,12},{20,16},{24,20},{28,24},{0,28},{5,1},{9... | collective-permute-start | bytes 147464 | tf_op jit(solution)/shard_map/ppermute | solution.py:18
  57.4 1.9 %collective-permute-done.4 = f32[48,2,128]{2,0,1:T(8,128)} collective-permute-done((f32[48,2,128]{2,0,1:T(8,128)S(1)}, f32[48,2,128]{2,0,1:T(8,128)}, u32[]{:S(2)}, u32[]{:S(2)}) %collective-permute-start.4) | collective-permute-done | bytes 49184 | tf_op jit(solution)/shard_map/ppermute | solution.py:15
  61.0 1.1 %fusion.49 = (f32[48,20,2]{2,0,1:T(8,128)}, f32[48,20,2]{2,0,1:T(8,128)}) fusion(f32[48,20,128]{2,0,1:T(8,128)S(1)} %constant_dynamic-update-slice_fusion), kind=kLoop, calls=%fused_computation.97 | loop fusion | bytes 30720 | tf_op jit(solution)/shard_map/slice | solution.py:16
  62.1 1.3 %copy.79 = f32[48,20,2]{0,1,2:T(8,128)S(1)} copy(f32[48,20,2]{2,0,1:T(8,128)} %get-tuple-element.39) | data formatting | bytes 15360 | tf_op jit(solution)/shard_map/slice | solution.py:16
  63.3 1.5 %collective-permute-start.6 = (f32[48,20,2]{0,1,2:T(8,128)S(1)}, f32[48,20,2]{0,1,2:T(8,128)S(1)}, u32[]{:S(2)}, u32[]{:S(2)}) collective-permute-start(f32[48,20,2]{0,1,2:T(8,128)S(1)} %copy.79), channel_id=1, source_target_pairs={{0,1},{1,2},{2,3},{3,0},{4,5},{5,6},{6,7},{7,4},{8,9},{9,10},{10,1... | collective-permute-start | bytes 23048 | tf_op jit(solution)/shard_map/ppermute | solution.py:15
  64.9 1.3 %copy.80 = f32[48,20,2]{0,1,2:T(8,128)S(1)} copy(f32[48,20,2]{2,0,1:T(8,128)} %get-tuple-element.40) | data formatting | bytes 15360 | tf_op jit(solution)/shard_map/slice | solution.py:18
  66.2 2.4 %collective-permute-start.7 = (f32[48,20,2]{0,1,2:T(8,128)S(1)}, f32[48,20,2]{0,1,2:T(8,128)S(1)}, u32[]{:S(2)}, u32[]{:S(2)}) collective-permute-start(f32[48,20,2]{0,1,2:T(8,128)S(1)} %copy.80), channel_id=1, source_target_pairs={{1,0},{2,1},{3,2},{0,3},{5,4},{6,5},{7,6},{4,7},{9,8},{10,9},{11,1... | collective-permute-start | bytes 23048 | tf_op jit(solution)/shard_map/ppermute | solution.py:18
  69.4 1.0 %copy.81 = f32[48,20,2]{2,0,1:T(8,128)} copy(f32[48,20,2]{0,1,2:T(8,128)S(1)} %collective-permute-done.6) | data formatting | bytes 15360 | tf_op jit(solution)/shard_map/ppermute | solution.py:15
  71.5 1.6 %maximum_multiply_fusion.1 = f32[48,20,132]{2,0,1:T(8,128)S(1)} fusion(f32[48,20,2]{2,0,1:T(8,128)} %copy.82, f32[48,20,128]{2,0,1:T(8,128)S(1)} %constant_dynamic-update-slice_fusion, f32[48,20,2]{2,0,1:T(8,128)} %copy.81, f32[20]{0:T(128)S(1)} %not_convert_fusion.1), kind=kLoop, calls=%fused_computation.25 | loop fusion | flops 380160 | bytes 1013840 | tf_op jit(solution)/shard_map/mul | solution.py:38
  74.2 1.2 %pad_maximum_fusion = f32[128,20,128]{0,1,2:T(8,128)S(1)} fusion(f32[128,2,128]{0,1,2:T(2,128)} %collective-permute-done.1, f32[128,16,128]{0,1,2:T(8,128)S(1)} %copy.67, f32[128,2,128]{0,1,2:T(2,128)} %collective-permute-done), kind=kLoop, calls=%fused_computation.2 | loop fusion | flops 655360 | bytes 2621440 | tf_op jit(solution)/shard_map/concatenate | solution.py:19
  75.4 1.3 %collective-permute-start.2 = (f32[128,20,2]{0,1,2:T(8,128)S(1)}, f32[128,20,2]{0,1,2:T(8,128)S(1)}, u32[]{:S(2)}, u32[]{:S(2)}) collective-permute-start(f32[128,20,2]{0,1,2:T(8,128)S(1)} %get-tuple-element.35), channel_id=1, source_target_pairs={{0,1},{1,2},{2,3},{3,0},{4,5},{5,6},{6,7},{7,4},{8,9},{9,10},{10,1... | collective-permute-start | bytes 61448 | tf_op jit(solution)/shard_map/ppermute | solution.py:15
  76.7 3.1 %collective-permute-start.3 = (f32[128,20,2]{0,1,2:T(8,128)S(1)}, f32[128,20,2]{0,1,2:T(8,128)S(1)}, u32[]{:S(2)}, u32[]{:S(2)}) collective-permute-start(f32[128,20,2]{0,1,2:T(8,128)S(1)} %get-tuple-element.36), channel_id=1, source_target_pairs={{1,0},{2,1},{3,2},{0,3},{5,4},{6,5},{7,6},{4,7},{9,8},{10,9},{11,1... | collective-permute-start | bytes 61448 | tf_op jit(solution)/shard_map/ppermute | solution.py:18
  84.0 1.3 %copy.75 = f32[16,8,128]{1,2,0:T(8,128)} copy(f32[16,8,128]{2,1,0:T(8,128)S(1)} %bitcast.54) | data formatting | bytes 131072 | tf_op jit(solution)/shard_map/reshape | solution.py:110
  85.4 2.3 %slice_add_fusion.3 = f32[8,16,128]{0,2,1:T(8,128)} fusion(f32[128,16,128]{0,2,1:T(8,128)S(1)} %fusion.16, f32[16,8,128]{1,2,0:T(8,128)} %copy.75), kind=kLoop, calls=%fused_computation.18 | loop fusion | flops 16384 | bytes 196608 | tf_op jit(solution)/shard_map/add | solution.py:116
  87.7 5.1 %scatter-add.6 = f32[128,16,128]{0,2,1:T(8,128)S(1)} dynamic-update-slice(f32[128,16,128]{0,2,1:T(8,128)S(1)} %fusion.16, f32[8,16,128]{0,2,1:T(8,128)} %slice_add_fusion.3, s32[]{:T(128)} %constant.113.clone.1, s32[]{:T(128)} %constant.113.clone.1, s32[]{:T(128)} %constant.113.clone.1) | dynamic-update-slice | bytes 131076 | tf_op jit(solution)/shard_map/scatter-add | solution.py:116
  92.8 1.4 %copy.83 = f32[128,16,128]{2,1,0:T(8,128)} copy(f32[128,16,128]{0,2,1:T(8,128)S(1)} %scatter-add.6) | data formatting | bytes 2097152
  (68 shorter events, 15.8 us)
Async XLA Ops:
  7.2 39.2 %copy-start = (bf16[1,48,128,128]{3,2,1,0:T(8,128)(2,1)S(1)}, bf16[1,48,128,128]{3,2,1,0:T(8,128)(2,1)}, u32[]{:S(2)}) copy-start(bf16[1,48,128,128]{3,2,1,0:T(8,128)(2,1)} %param.20) | copy-start | bytes 4718596
  7.2 7.1 %copy-start.8 = (s32[1,48]{1,0:T(1,128)S(1)}, s32[1,48]{1,0:T(1,128)}, u32[]{:S(2)}) copy-start(s32[1,48]{1,0:T(1,128)} %param.21) | copy-start | bytes 580
  7.2 7.1 %copy-start.6 = (s32[1,48]{1,0:T(1,128)S(1)}, s32[1,48]{1,0:T(1,128)}, u32[]{:S(2)}) copy-start(s32[1,48]{1,0:T(1,128)} %param.22) | copy-start | bytes 580
  7.2 22.7 %copy-start.1 = (f32[48,16,128]{2,1,0:T(8,128)S(1)}, f32[48,16,128]{2,1,0:T(8,128)}, u32[]{:S(2)}) copy-start(f32[48,16,128]{2,1,0:T(8,128)} %param.16) | copy-start | bytes 1179652
  7.2 22.9 %copy-start.7 = (s32[16,1]{0,1:T(1,128)S(1)}, s32[16,1]{0,1:T(1,128)}, u32[]{:S(2)}) copy-start(s32[16,1]{0,1:T(1,128)} %param.19) | copy-start | bytes 196
  7.2 75.9 %reduce-scatter.2.cloned.1.call-start = ((), (), s32[]{:S(2)}) async-start(), calls=%async_computation.1 | async-start | bytes 655360 | tf_op jit(solution)/shard_map/reduce_scatter | solution.py:96
  10.1 64.1 %collective-permute-start = (f32[128,2,128]{0,1,2:T(2,128)}, f32[128,2,128]{0,1,2:T(2,128)}, u32[]{:S(2)}, u32[]{:S(2)}) collective-permute-start(f32[128,2,128]{0,1,2:T(2,128)} %get-tuple-element.37), channel_id=1, source_target_pairs={{0,4},{4,8},{8,12},{12,16},{16,20},{20,24},{24,28},{28,0},{1,5},{5... | collective-permute-start | bytes 393224 | tf_op jit(solution)/shard_map/ppermute | solution.py:15
  10.6 63.6 %collective-permute-start.1 = (f32[128,2,128]{0,1,2:T(2,128)}, f32[128,2,128]{0,1,2:T(2,128)}, u32[]{:S(2)}, u32[]{:S(2)}) collective-permute-start(f32[128,2,128]{0,1,2:T(2,128)} %get-tuple-element.38), channel_id=1, source_target_pairs={{4,0},{8,4},{12,8},{16,12},{20,16},{24,20},{28,24},{0,28},{5,1},{9... | collective-permute-start | bytes 393224 | tf_op jit(solution)/shard_map/ppermute | solution.py:18
  30.1 0.7 copy-start.2
  46.4 0.6 copy-start.5
  54.8 4.5 %collective-permute-start.4 = (f32[48,2,128]{2,0,1:T(8,128)S(1)}, f32[48,2,128]{2,0,1:T(8,128)}, u32[]{:S(2)}, u32[]{:S(2)}) collective-permute-start(f32[48,2,128]{2,0,1:T(8,128)S(1)} %get-tuple-element.42), channel_id=1, source_target_pairs={{0,4},{4,8},{8,12},{12,16},{16,20},{20,24},{24,28},{28,0},{1,5},{5... | collective-permute-start | bytes 147464 | tf_op jit(solution)/shard_map/ppermute | solution.py:15
  54.8 5.4 %collective-permute-start.5 = (f32[48,2,128]{2,0,1:T(8,128)}, f32[48,2,128]{2,0,1:T(8,128)}, u32[]{:S(2)}, u32[]{:S(2)}) collective-permute-start(f32[48,2,128]{2,0,1:T(8,128)} %get-tuple-element.41), channel_id=1, source_target_pairs={{4,0},{8,4},{12,8},{16,12},{20,16},{24,20},{28,24},{0,28},{5,1},{9... | collective-permute-start | bytes 147464 | tf_op jit(solution)/shard_map/ppermute | solution.py:18
  63.3 6.0 %collective-permute-start.6 = (f32[48,20,2]{0,1,2:T(8,128)S(1)}, f32[48,20,2]{0,1,2:T(8,128)S(1)}, u32[]{:S(2)}, u32[]{:S(2)}) collective-permute-start(f32[48,20,2]{0,1,2:T(8,128)S(1)} %copy.79), channel_id=1, source_target_pairs={{0,1},{1,2},{2,3},{3,0},{4,5},{5,6},{6,7},{7,4},{8,9},{9,10},{10,1... | collective-permute-start | bytes 23048 | tf_op jit(solution)/shard_map/ppermute | solution.py:15
  66.2 4.3 %collective-permute-start.7 = (f32[48,20,2]{0,1,2:T(8,128)S(1)}, f32[48,20,2]{0,1,2:T(8,128)S(1)}, u32[]{:S(2)}, u32[]{:S(2)}) collective-permute-start(f32[48,20,2]{0,1,2:T(8,128)S(1)} %copy.80), channel_id=1, source_target_pairs={{1,0},{2,1},{3,2},{0,3},{5,4},{6,5},{7,6},{4,7},{9,8},{10,9},{11,1... | collective-permute-start | bytes 23048 | tf_op jit(solution)/shard_map/ppermute | solution.py:18
  70.4 2.7 %copy-start.3 = (f32[48]{0:T(128)S(1)}, f32[48]{0:T(128)}, u32[]{:S(2)}) copy-start(f32[48]{0:T(128)} %param.18) | copy-start | bytes 580
  75.4 6.1 %collective-permute-start.2 = (f32[128,20,2]{0,1,2:T(8,128)S(1)}, f32[128,20,2]{0,1,2:T(8,128)S(1)}, u32[]{:S(2)}, u32[]{:S(2)}) collective-permute-start(f32[128,20,2]{0,1,2:T(8,128)S(1)} %get-tuple-element.35), channel_id=1, source_target_pairs={{0,1},{1,2},{2,3},{3,0},{4,5},{5,6},{6,7},{7,4},{8,9},{9,10},{10,1... | collective-permute-start | bytes 61448 | tf_op jit(solution)/shard_map/ppermute | solution.py:15
  76.7 4.9 %collective-permute-start.3 = (f32[128,20,2]{0,1,2:T(8,128)S(1)}, f32[128,20,2]{0,1,2:T(8,128)S(1)}, u32[]{:S(2)}, u32[]{:S(2)}) collective-permute-start(f32[128,20,2]{0,1,2:T(8,128)S(1)} %get-tuple-element.36), channel_id=1, source_target_pairs={{1,0},{2,1},{3,2},{0,3},{5,4},{6,5},{7,6},{4,7},{9,8},{10,9},{11,1... | collective-permute-start | bytes 61448 | tf_op jit(solution)/shard_map/ppermute | solution.py:18
  81.6 0.7 copy-start.4
Sparse Core Ops, SparseCore 0:
  53.4 22.3 reduce-scatter.1
where the time goes:
time: 103 us; the launch traced here: 102 us
  blocking collectives  28.6 us (28%)
  local copies, waits for them, and re-layouts  26.5 us (26%)
  between operations  15 us (15%)
  starting transfers between devices  14.4 us (14%)
  other arithmetic  9.11 us (9%)
  matrix products  4.66 us (5%)
  waiting for transfers between devices  3.77 us (4%)
    all_gather x1, blocking collectives, shards(): lax.all_gather(atm_source, 'tile', axis=1, tiled=True)  14.4 us
    all_gather x1, blocking collectives, shards(): lax.all_gather(ocean_source, 'tile', axis=1, tiled=True)  14.3 us
    ppermute x4, starting transfers between devices, padded_2(): lax.ppermute(lax.slice_in_dim(block, 0, width, axis=dim), axis, backward)  11 us
    unnamed x28, local copies, waits for them, and re-layouts  7.44 us
    scatter-add x1, local copies, waits for them, and re-layouts, shards(): atm_next = atm_stepped.at[:SURF].add(jnp.transpose(atm_force, (1, 0, 2)))  5.1 us
    ppermute x4, waiting for transfers between devices, padded_2(): lax.ppermute(lax.slice_in_dim(block, block.shape[dim] - width, None, axis...  3.67 us
    mul x4, other arithmetic, ghosts(): return padded * retain[None, :, None]  3.33 us
    ppermute x4, starting transfers between devices, padded_2(): lax.ppermute(lax.slice_in_dim(block, block.shape[dim] - width, None, axis...  3.33 us
  transfers between devices with their start and end apart: 9, of which 4 were waited for; matrix products, arithmetic and copies ran while one was open for 24% of the time, Pallas kernels for 0%

commit v1 on v0

--- a/solution.py
+++ b/solution.py
@@ -4,6 +4,11 @@
 from jax.sharding import PartitionSpec as P
 
 SURF = 8
+
+
+def swapped_in(block, axis, dim):
+    sent = jnp.stack([block] * lax.axis_size(axis))
+    return jnp.concatenate(lax.all_to_all(sent, axis, 0, 0), axis=dim)
 
 
 def padded_2(block, sides, width):
@@ -57,7 +62,7 @@
     atm_source = atm_state[:SURF].astype(jnp.bfloat16)
     ocean_source = (ocean_state[:SURF] * wet_rows[None, :, None]).astype(jnp.bfloat16)
     atm_band, ocean_band = (
-        lax.all_gather(atm_source, "tile", axis=1, tiled=True),
+        swapped_in(atm_source, "tile", 1),
         lax.all_gather(ocean_source, "tile", axis=1, tiled=True),
     )
     anchor = pair_src[0]

time: 103 us -> 112 us (1.087)
  blocking collectives: 28.6 us -> 14 us
  waiting for transfers between devices: 3.77 us -> 17.2 us
  starting transfers between devices: 14.4 us -> 19.7 us
  other arithmetic: 9.11 us -> 12.8 us
    reduce_scatter x1, waiting for transfers between devices: 0.02 us -> 16.7 us  [shards(): lax.psum_scatter(jnp.dot(ahead_hot, ahead_flat, precision=lax.Precision.H...]
    all_gather x1 -> x0, blocking collectives: 14.4 us -> none  [shards(): lax.all_gather(atm_source, 'tile', axis=1, tiled=True)]
    all_to_all x0 -> x1, starting transfers between devices: none -> 5.63 us  [swapped_in(): return jnp.concatenate(lax.all_to_all(sent, axis, 0, 0), axis=dim)]
    ppermute x4, waiting for transfers between devices: 3.67 us -> 0.49 us  [padded_2(): lax.ppermute(lax.slice_in_dim(block, block.shape[dim] - width, None, axis...]
    gather x1, local copies, waits for them, and re-layouts: 2.15 us -> 0.61 us  [shards(): jnp.take(ocean_band, target, axis=1)]
    unnamed x28 -> x49, local copies, waits for them, and re-layouts: 7.44 us -> 8.48 us
  transfers between devices with their start and end apart: 9 -> 10, of which waited for: 4 -> 2; matrix products, arithmetic and copies ran while one was open for 24% -> 25% of each run, Pallas kernels for 0% -> 0%
where the time goes in v1:
time: 112 us; the launch traced here: 111 us
  local copies, waits for them, and re-layouts  27 us (24%)
  starting transfers between devices  19.7 us (18%)
  waiting for transfers between devices  17.2 us (15%)
  between operations  15.1 us (13%)
  blocking collectives  14 us (12%)
  other arithmetic  12.8 us (11%)
  matrix products  5.02 us (4%)
    reduce_scatter x1, waiting for transfers between devices, shards(): lax.psum_scatter(jnp.dot(ahead_hot, ahead_flat, precision=lax.Precision.H...  16.7 us
    all_gather x1, blocking collectives, shards(): lax.all_gather(ocean_source, 'tile', axis=1, tiled=True)  14 us
    ppermute x4, starting transfers between devices, padded_2(): lax.ppermute(lax.slice_in_dim(block, 0, width, axis=dim), axis, backward)  11.4 us
    unnamed x49, local copies, waits for them, and re-layouts  8.48 us
    all_to_all x1, starting transfers between devices, swapped_in(): return jnp.concatenate(lax.all_to_all(sent, axis, 0, 0), axis=dim)  5.63 us
    scatter-add x1, local copies, waits for them, and re-layouts, shards(): atm_next = atm_stepped.at[:SURF].add(jnp.transpose(atm_force, (1, 0, 2)))  5.1 us
    mul x4, other arithmetic, ghosts(): return padded * retain[None, :, None]  3.33 us
    slice x4, local copies, waits for them, and re-layouts, padded_2(): lax.slice_in_dim(block, block.shape[dim] - width, None, axis=dim)  3.13 us
  transfers between devices with their start and end apart: 10, of which 2 were waited for; matrix products, arithmetic and copies ran while one was open for 25% of the time, Pallas kernels for 0%

profile of v1, /device:TPU:0, one launch (start us, length us, event | category | flops | bytes accessed | tf_op | source)
XLA Modules:
  0.0 110.7 jit_solution(16397477024628191455)
XLA Ops:
  7.2 2.0 %copy.69 = f32[128,16,128]{0,1,2:T(8,128)S(1)} copy(f32[128,16,128]{2,1,0:T(8,128)} %param.15) | data formatting | bytes 2097152 | tf_op args[0]
  10.5 2.9 %collective-permute-start.1 = (f32[128,2,128]{0,1,2:T(2,128)}, f32[128,2,128]{0,1,2:T(2,128)}, u32[]{:S(2)}, u32[]{:S(2)}) collective-permute-start(f32[128,2,128]{0,1,2:T(2,128)} %get-tuple-element.38), channel_id=1, source_target_pairs={{4,0},{8,4},{12,8},{16,12},{20,16},{24,20},{28,24},{0,28},{5,1},{9... | collective-permute-start | bytes 393224 | tf_op jit(solution)/shard_map/ppermute | solution.py:23
  14.9 5.6 %all-to-all-start = ((bf16[4,8,16,128]{3,2,1,0:T(8,128)(2,1)}), bf16[4,8,16,128]{3,2,1,0:T(8,128)(2,1)}, u32[]{:S(2)}, u32[]{:S(2)}) async-start(bf16[4,8,16,128]{3,2,1,0:T(8,128)(2,1)} %stack.2), calls=%async_computation | async-start | bytes 262144 | tf_op jit(solution)/shard_map/all_to_all | solution.py:11
  21.3 2.6 %collective-permute-start.5 = (f32[48,2,128]{2,0,1:T(8,128)}, f32[48,2,128]{2,0,1:T(8,128)S(1)}, u32[]{:S(2)}, u32[]{:S(2)}) collective-permute-start(f32[48,2,128]{2,0,1:T(8,128)} %get-tuple-element.41), channel_id=1, source_target_pairs={{4,0},{8,4},{12,8},{16,12},{20,16},{24,20},{28,24},{0,28},{5,1},{9... | collective-permute-start | bytes 147464 | tf_op jit(solution)/shard_map/ppermute | solution.py:23
  25.8 14.0 %all_gather.3 = bf16[8,64,128]{2,0,1:T(8,128)(2,1)S(1)} all-gather(bf16[8,16,128]{2,0,1:T(8,128)(2,1)S(1)} %fusion.36), channel_id=1, replica_groups=mesh['comp'=8,'tile'=4] {'tile'}, dimensions={1}, use_global_device_ids=true | all-gather | bytes 163840 | tf_op jit(solution)/shard_map/all_gather | solution.py:66
  40.4 1.2 %fusion.43 = s32[48]{0:T(128)} fusion(s32[1,48]{1,0:T(1,128)} %param.22, s32[]{:T(128)} %bitcast.52), kind=kLoop, calls=%fused_computation.90 | loop fusion | flops 1152 | bytes 388 | tf_op jit(solution)/shard_map/eq | solution.py:99
  41.5 1.2 %fusion.44 = s32[48]{0:T(128)} fusion(s32[1,48]{1,0:T(1,128)} %param.21, s32[]{:T(128)} %bitcast.54), kind=kLoop, calls=%fused_computation.91 | loop fusion | flops 1104 | bytes 388 | tf_op jit(solution)/shard_map/eq | solution.py:100
  43.3 1.6 %fusion.11 = f32[48,8,128]{2,1,0:T(8,128)} fusion(bf16[1,48,128,128]{3,2,1,0:T(8,128)(2,1)S(1)} %copy-done, bf16[48,8,128]{2,1,0:T(8,128)(2,1)S(1)} %gather_fusion.1, f32[48]{0:T(128)S(1)} %get-tuple-element.46, pred[48]{0:T(512)(128)(4,1)S(1)} %get-tuple-element.45), kind=kOutput, calls=%fused_computation.17 | convolution fusion | flops 12681216 | bytes 1868016 | tf_op jit(solution)/shard_map/fps,pts->pft/dot_general | solution.py:83
  47.6 1.3 %copy.82 = f32[48,20,2]{0,1,2:T(8,128)S(1)} copy(f32[48,20,2]{2,0,1:T(8,128)} %get-tuple-element.39) | data formatting | bytes 15360 | tf_op jit(solution)/shard_map/slice | solution.py:21
  48.9 1.4 %collective-permute-start.6 = (f32[48,20,2]{0,1,2:T(8,128)S(1)}, f32[48,20,2]{0,1,2:T(8,128)S(1)}, u32[]{:S(2)}, u32[]{:S(2)}) collective-permute-start(f32[48,20,2]{0,1,2:T(8,128)S(1)} %copy.82), channel_id=1, source_target_pairs={{0,1},{1,2},{2,3},{3,0},{4,5},{5,6},{6,7},{7,4},{8,9},{9,10},{10,1... | collective-permute-start | bytes 23048 | tf_op jit(solution)/shard_map/ppermute | solution.py:20
  50.3 1.3 %copy.83 = f32[48,20,2]{0,1,2:T(8,128)S(1)} copy(f32[48,20,2]{2,0,1:T(8,128)} %get-tuple-element.40) | data formatting | bytes 15360 | tf_op jit(solution)/shard_map/slice | solution.py:23
  51.5 2.5 %collective-permute-start.7 = (f32[48,20,2]{0,1,2:T(8,128)S(1)}, f32[48,20,2]{0,1,2:T(8,128)S(1)}, u32[]{:S(2)}, u32[]{:S(2)}) collective-permute-start(f32[48,20,2]{0,1,2:T(8,128)S(1)} %copy.83), channel_id=1, source_target_pairs={{1,0},{2,1},{3,2},{0,3},{5,4},{6,5},{7,6},{4,7},{9,8},{10,9},{11,1... | collective-permute-start | bytes 23048 | tf_op jit(solution)/shard_map/ppermute | solution.py:23
  56.6 1.6 %maximum_multiply_fusion.1 = f32[48,20,132]{2,0,1:T(8,128)S(1)} fusion(f32[48,20,2]{2,0,1:T(8,128)} %copy.85, f32[48,20,128]{2,0,1:T(8,128)S(1)} %constant_dynamic-update-slice_fusion, f32[48,20,2]{2,0,1:T(8,128)} %copy.84, f32[20]{0:T(128)S(1)} %copy-done.14), kind=kLoop, calls=%fused_computation.25 | loop fusion | flops 380160 | bytes 1013840 | tf_op jit(solution)/shard_map/mul | solution.py:43
  59.3 1.2 %pad_maximum_fusion = f32[128,20,128]{0,1,2:T(8,128)S(1)} fusion(f32[128,2,128]{0,1,2:T(2,128)} %collective-permute-done.1, f32[128,16,128]{0,1,2:T(8,128)S(1)} %copy.69, f32[128,2,128]{0,1,2:T(2,128)} %collective-permute-done), kind=kLoop, calls=%fused_computation.2 | loop fusion | flops 655360 | bytes 2621440 | tf_op jit(solution)/shard_map/concatenate | solution.py:24
  60.5 1.2 %copy-done.1 = f32[128,20,128]{0,1,2:T(8,128)} copy-done((f32[128,20,128]{0,1,2:T(8,128)}, f32[128,20,128]{0,1,2:T(8,128)S(1)}, u32[]{:S(2)}) %copy-start.1) | copy-done | bytes 1310744
  62.5 3.4 %collective-permute-start.3 = (f32[128,20,2]{0,1,2:T(8,128)S(1)}, f32[128,20,2]{0,1,2:T(8,128)S(1)}, u32[]{:S(2)}, u32[]{:S(2)}) collective-permute-start(f32[128,20,2]{0,1,2:T(8,128)S(1)} %get-tuple-element.36), channel_id=1, source_target_pairs={{1,0},{2,1},{3,2},{0,3},{5,4},{6,5},{7,6},{4,7},{9,8},{10,9},{11,1... | collective-permute-start | bytes 61448 | tf_op jit(solution)/shard_map/ppermute | solution.py:23
  67.7 1.2 %fusion.8 = f32[48,8,128]{2,1,0:T(8,128)S(1)} fusion(bf16[1,48,128,128]{3,2,1,0:T(8,128)(2,1)S(1)} %copy-done, bf16[48,8,128]{2,1,0:T(8,128)(2,1)S(1)} %gather_fusion, f32[48]{0:T(128)} %copy-done.6, pred[48]{0:T(512)(128)(4,1)} %compare_and_fusion.1), kind=kOutput, calls=%fused_computation.16 | convolution fusion | flops 12681216 | bytes 1868016 | tf_op jit(solution)/shard_map/fpt,pts->pfs/dot_general | solution.py:74
  70.0 1.2 %convolution_add_fusion = f32[128,1024]{1,0:T(8,128)} fusion(f32[128,1024]{1,0:T(8,128)S(1)} %fusion.26, f32[6,8,8,128]{3,2,1,0:T(8,128)S(1)} %bitcast.55, s32[48]{0:T(128)S(1)} %copy-done.16), kind=kOutput, calls=%fused_computation.15 | convolution fusion | flops 75634688 | bytes 1245376 | tf_op jit(solution)/shard_map/dot_general | solution.py:108
  71.2 1.2 %fusion.23 = f32[48,16,128]{2,0,1:T(8,128)} fusion(f32[48,18,130]{2,0,1:T(8,128)S(1)} %fusion.20, f32[48]{0:T(128)S(1)} %copy-done.8), kind=kLoop, calls=%fused_computation.36 | loop fusion | flops 688128 | bytes 2359488 | tf_op jit(solution)/shard_map/add | solution.py:33
  75.2 16.7 %reduce-scatter.2.cloned.1.call-done = f32[32,1024]{1,0:T(8,128)} async-done(((f32[128,1024]{1,0:T(8,128)}), f32[32,1024]{1,0:T(8,128)}) %reduce-scatter.2.cloned.1.call-update) | async-done | bytes 131088 | tf_op jit(solution)/shard_map/reduce_scatter | solution.py:101
  92.8 1.3 %copy.78 = f32[16,8,128]{1,2,0:T(8,128)} copy(f32[16,8,128]{2,1,0:T(8,128)S(1)} %bitcast.58) | data formatting | bytes 131072 | tf_op jit(solution)/shard_map/reshape | solution.py:115
  94.1 2.3 %slice_add_fusion.3 = f32[8,16,128]{0,2,1:T(8,128)} fusion(f32[128,16,128]{0,2,1:T(8,128)S(1)} %fusion.16, f32[16,8,128]{1,2,0:T(8,128)} %copy.78), kind=kLoop, calls=%fused_computation.18 | loop fusion | flops 16384 | bytes 196608 | tf_op jit(solution)/shard_map/add | solution.py:121
  96.4 5.1 %scatter-add.6 = f32[128,16,128]{0,2,1:T(8,128)S(1)} dynamic-update-slice(f32[128,16,128]{0,2,1:T(8,128)S(1)} %fusion.16, f32[8,16,128]{0,2,1:T(8,128)} %slice_add_fusion.3, s32[]{:T(128)} %constant.113.clone.1, s32[]{:T(128)} %constant.113.clone.1, s32[]{:T(128)} %constant.113.clone.1) | dynamic-update-slice | bytes 131076 | tf_op jit(solution)/shard_map/scatter-add | solution.py:121
  101.5 1.4 %copy.86 = f32[128,16,128]{2,1,0:T(8,128)} copy(f32[128,16,128]{0,2,1:T(8,128)S(1)} %scatter-add.6) | data formatting | bytes 2097152
  (92 shorter events, 20.3 us)
Async XLA Ops:
  7.2 36.2 %copy-start = (bf16[1,48,128,128]{3,2,1,0:T(8,128)(2,1)S(1)}, bf16[1,48,128,128]{3,2,1,0:T(8,128)(2,1)}, u32[]{:S(2)}) copy-start(bf16[1,48,128,128]{3,2,1,0:T(8,128)(2,1)} %param.20) | copy-start | bytes 4718596
  7.2 13.3 %copy-start.4 = (f32[48,16,128]{2,1,0:T(8,128)S(1)}, f32[48,16,128]{2,1,0:T(8,128)}, u32[]{:S(2)}) copy-start(f32[48,16,128]{2,1,0:T(8,128)} %param.16) | copy-start | bytes 1179652
  9.2 14.8 %copy-start.19 = (s32[1,48]{1,0:T(1,128)S(1)}, s32[1,48]{1,0:T(1,128)}, u32[]{:S(2)}) copy-start(s32[1,48]{1,0:T(1,128)} %param.21) | copy-start | bytes 580
  9.2 15.9 %copy-start.17 = (s32[1,48]{1,0:T(1,128)S(1)}, s32[1,48]{1,0:T(1,128)}, u32[]{:S(2)}) copy-start(s32[1,48]{1,0:T(1,128)} %param.22) | copy-start | bytes 580
  9.2 16.0 %copy-start.18 = (s32[16,1]{0,1:T(1,128)S(1)}, s32[16,1]{0,1:T(1,128)}, u32[]{:S(2)}) copy-start(s32[16,1]{0,1:T(1,128)} %param.19) | copy-start | bytes 196
  10.0 49.3 %collective-permute-start = (f32[128,2,128]{0,1,2:T(2,128)}, f32[128,2,128]{0,1,2:T(2,128)}, u32[]{:S(2)}, u32[]{:S(2)}) collective-permute-start(f32[128,2,128]{0,1,2:T(2,128)} %get-tuple-element.37), channel_id=1, source_target_pairs={{0,4},{4,8},{8,12},{12,16},{16,20},{20,24},{24,28},{28,0},{1,5},{5... | collective-permute-start | bytes 393224 | tf_op jit(solution)/shard_map/ppermute | solution.py:20
  10.5 48.8 %collective-permute-start.1 = (f32[128,2,128]{0,1,2:T(2,128)}, f32[128,2,128]{0,1,2:T(2,128)}, u32[]{:S(2)}, u32[]{:S(2)}) collective-permute-start(f32[128,2,128]{0,1,2:T(2,128)} %get-tuple-element.38), channel_id=1, source_target_pairs={{4,0},{8,4},{12,8},{16,12},{20,16},{24,20},{28,24},{0,28},{5,1},{9... | collective-permute-start | bytes 393224 | tf_op jit(solution)/shard_map/ppermute | solution.py:23
  14.9 50.9 %all-to-all-start = ((bf16[4,8,16,128]{3,2,1,0:T(8,128)(2,1)}), bf16[4,8,16,128]{3,2,1,0:T(8,128)(2,1)}, u32[]{:S(2)}, u32[]{:S(2)}) async-start(bf16[4,8,16,128]{3,2,1,0:T(8,128)(2,1)} %stack.2), calls=%async_computation | async-start | bytes 262144 | tf_op jit(solution)/shard_map/all_to_all | solution.py:11
  20.5 71.3 %reduce-scatter.2.cloned.1.call-start = ((), (), s32[]{:S(2)}) async-start(), calls=%async_computation.2 | async-start | bytes 655360 | tf_op jit(solution)/shard_map/reduce_scatter | solution.py:101
  21.3 24.3 %collective-permute-start.4 = (f32[48,2,128]{2,0,1:T(8,128)S(1)}, f32[48,2,128]{2,0,1:T(8,128)}, u32[]{:S(2)}, u32[]{:S(2)}) collective-permute-start(f32[48,2,128]{2,0,1:T(8,128)S(1)} %get-tuple-element.42), channel_id=1, source_target_pairs={{0,4},{4,8},{8,12},{12,16},{16,20},{20,24},{24,28},{28,0},{1,5},{5... | collective-permute-start | bytes 147464 | tf_op jit(solution)/shard_map/ppermute | solution.py:20
  21.3 25.2 %collective-permute-start.5 = (f32[48,2,128]{2,0,1:T(8,128)}, f32[48,2,128]{2,0,1:T(8,128)S(1)}, u32[]{:S(2)}, u32[]{:S(2)}) collective-permute-start(f32[48,2,128]{2,0,1:T(8,128)} %get-tuple-element.41), channel_id=1, source_target_pairs={{4,0},{8,4},{12,8},{16,12},{20,16},{24,20},{28,24},{0,28},{5,1},{9... | collective-permute-start | bytes 147464 | tf_op jit(solution)/shard_map/ppermute | solution.py:23
  25.2 20.4 %copy-start.6 = (f32[48]{0:T(128)}, f32[48]{0:T(128)S(1)}, u32[]{:S(2)}) copy-start(f32[48]{0:T(128)S(1)} %get-tuple-element.46) | copy-start | bytes 580
  47.6 9.0 %copy-start.14 = (f32[20]{0:T(128)S(1)}, f32[20]{0:T(128)}, u32[]{:S(2)}) copy-start(f32[20]{0:T(128)} %not_convert_fusion.1) | copy-start | bytes 244
  48.9 5.7 %collective-permute-start.6 = (f32[48,20,2]{0,1,2:T(8,128)S(1)}, f32[48,20,2]{0,1,2:T(8,128)S(1)}, u32[]{:S(2)}, u32[]{:S(2)}) collective-permute-start(f32[48,20,2]{0,1,2:T(8,128)S(1)} %copy.82), channel_id=1, source_target_pairs={{0,1},{1,2},{2,3},{3,0},{4,5},{5,6},{6,7},{7,4},{8,9},{9,10},{10,1... | collective-permute-start | bytes 23048 | tf_op jit(solution)/shard_map/ppermute | solution.py:20
  51.5 4.0 %collective-permute-start.7 = (f32[48,20,2]{0,1,2:T(8,128)S(1)}, f32[48,20,2]{0,1,2:T(8,128)S(1)}, u32[]{:S(2)}, u32[]{:S(2)}) collective-permute-start(f32[48,20,2]{0,1,2:T(8,128)S(1)} %copy.83), channel_id=1, source_target_pairs={{1,0},{2,1},{3,2},{0,3},{5,4},{6,5},{7,6},{4,7},{9,8},{10,9},{11,1... | collective-permute-start | bytes 23048 | tf_op jit(solution)/shard_map/ppermute | solution.py:23
  54.1 4.2 %copy-start.12 = (f32[18]{0:T(128)}, f32[18]{0:T(128)S(1)}, u32[]{:S(2)}) copy-start(f32[18]{0:T(128)S(1)} %not_convert_fusion) | copy-start | bytes 220
  55.6 2.7 %copy-start.7 = (f32[48]{0:T(128)S(1)}, f32[48]{0:T(128)}, u32[]{:S(2)}) copy-start(f32[48]{0:T(128)} %param.18) | copy-start | bytes 580
  61.7 11.2 %collective-permute-start.2 = (f32[128,20,2]{0,1,2:T(8,128)S(1)}, f32[128,20,2]{0,1,2:T(8,128)}, u32[]{:S(2)}, u32[]{:S(2)}) collective-permute-start(f32[128,20,2]{0,1,2:T(8,128)S(1)} %get-tuple-element.35), channel_id=1, source_target_pairs={{0,1},{1,2},{2,3},{3,0},{4,5},{5,6},{6,7},{7,4},{8,9},{9,10},{10,1... | collective-permute-start | bytes 61448 | tf_op jit(solution)/shard_map/ppermute | solution.py:20
  62.5 11.2 %collective-permute-start.3 = (f32[128,20,2]{0,1,2:T(8,128)S(1)}, f32[128,20,2]{0,1,2:T(8,128)S(1)}, u32[]{:S(2)}, u32[]{:S(2)}) collective-permute-start(f32[128,20,2]{0,1,2:T(8,128)S(1)} %get-tuple-element.36), channel_id=1, source_target_pairs={{1,0},{2,1},{3,2},{0,3},{5,4},{6,5},{7,6},{4,7},{9,8},{10,9},{11,1... | collective-permute-start | bytes 61448 | tf_op jit(solution)/shard_map/ppermute | solution.py:23
  66.8 3.1 %copy-start.5 = (f32[48,8,128]{2,1,0:T(8,128)S(1)}, f32[48,8,128]{2,1,0:T(8,128)}, u32[]{:S(2)}) copy-start(f32[48,8,128]{2,1,0:T(8,128)} %fusion.11) | copy-start | bytes 589828
  66.9 3.1 %copy-start.16 = (s32[48]{0:T(128)S(1)}, s32[48]{0:T(128)}, u32[]{:S(2)}) copy-start(s32[48]{0:T(128)} %fusion.44) | copy-start | bytes 580
  68.9 2.2 %copy-start.8 = (f32[48]{0:T(128)S(1)}, f32[48]{0:T(128)}, u32[]{:S(2)}) copy-start(f32[48]{0:T(128)} %param.18) | copy-start | bytes 580
  101.5 1.4 %copy-start.3 = (f32[48,16,128]{2,0,1:T(8,128)S(1)}, f32[48,16,128]{2,0,1:T(8,128)}, u32[]{:S(2)}) copy-start(f32[48,16,128]{2,0,1:T(8,128)} %fusion.23) | copy-start | bytes 1179652
  101.5 1.4 %copy-start.11 = (f32[16]{0:T(128)S(1)}, f32[16]{0:T(128)}, u32[]{:S(2)}) copy-start(f32[16]{0:T(128)} %copy-done.10) | copy-start | bytes 196
  (6 other events, 5.5 us)
Sparse Core Ops, SparseCore 0:
  71.3 20.5 reduce-scatter.1
